TPU v7x, 32 devices: a whole 2x2x4 slice. The times are simulated.
32 devices in a mesh: seg: 4 (over y, core), ep: 8 (over z, x).
Axes of the slice: x: 2, y: 2, z: 4, core: 2. Of those that a mesh axis runs over, the one named last changes fastest.
Arguments:
- queries: bfloat16 [2048, 2048], P(('seg', 'ep')), may hold values from -6 to 6
- keys: bfloat16 [2048, 2048], P(('seg', 'ep')), may hold values from -1.25 to 1.25
- values: bfloat16 [2048, 2048], P(('seg', 'ep')), may hold values from -54 to 54
- log_decay: float32 [2048, 16], P('seg', 'ep'), may hold values from -1 to 0
- out_gain: float32 [2048], replicated, may hold values from 0.1 to 1.9
- out_proj: bfloat16 [2048, 6144], P('ep', 'seg'), may hold values from -0.125 to 0.125
- experts: int32 [256, 2], P(('seg', 'ep')), may hold values from 0 to 3, all different within a row; in each aligned block of 8 rows (0 to 7, 8 to 15, ...) at most 8 rows name the same one
- gates: float32 [256, 2], P(('seg', 'ep')), may hold values from 0.2 to 1
- up_weight: bfloat16 [8, 6144, 2304], P('ep', None, 'seg'), may hold values from -0.078125 to 0.078125
- down_weight: bfloat16 [8, 2304, 6144], P('ep', 'seg'), may hold values from -0.09375 to 0.09375
Outputs:
- attn_out: bfloat16 [2048, 2048], P(('seg', 'ep'))
- moe_out: bfloat16 [256, 6144], P(('seg', 'ep'))
Inputs may be any that keep to these rules, and one draw needn't show every extreme that they name: Each row names two different experts. The 8 rows of one device name any one expert at most 8 times, and in some devices one expert exactly 8 times.
All inputs are finite; a program needn't handle non-finite values.
Results may differ from a plain program's by a relative error of at most 0.025.
Values may be sent and summed in bfloat16 or wider, within the bound.
A program may use at most 128 MiB of HBM per device.

v0:
```python
import math
import jax
import jax.numpy as jnp
from jax import lax
from jax.sharding import PartitionSpec as P

epsilon = 1e-06


def prefix(x, axis, join, neutral):
    place = lax.axis_index(axis)
    gathered = jax.tree.map(
        lambda a, kind: lax.all_gather(a.astype(kind), axis), x, (jnp.bfloat16, jnp.bfloat16)
    )
    state = jax.tree.map(lambda a, e: jnp.zeros_like(a) + jnp.asarray(e, a.dtype), x, neutral)

    def one(turn, state):
        return join(
            state,
            jax.tree.map(
                lambda a, own: lax.dynamic_index_in_dim(a, turn, 0, False).astype(own.dtype),
                gathered,
                x,
            ),
        )

    return lax.fori_loop(0, place, one, state)


def chain_combine(first_part, second_part):
    return (
        first_part[0] * second_part[0],
        second_part[0][:, None, None] * first_part[1] + second_part[1],
    )


def route_tables(experts, gates, expert_count, capacity):
    token_count = experts.shape[0]
    flattened = experts.reshape(-1)
    onehot = (flattened[:, None] == jnp.arange(expert_count, dtype=jnp.int32)[None, :]).astype(
        jnp.int32
    )
    earlier = jnp.cumsum(onehot, axis=0) - onehot
    position = jnp.sum(earlier * onehot, axis=1)
    slot_index = (flattened * capacity + position).reshape(token_count, 2)
    columns = jnp.arange(expert_count * capacity, dtype=jnp.int32)
    matches = slot_index[:, :, None] == columns[None, None, :]
    dispatch = jnp.any(matches, axis=1).T.astype(jnp.bfloat16)
    combine = jnp.sum(jnp.where(matches, gates[:, :, None], 0.0), axis=1)
    return (dispatch, combine)


def expert_output(row_data, up_piece, down_piece):
    hidden = jax.nn.silu(jnp.dot(row_data, up_piece, preferred_element_type=jnp.float32)).astype(
        jnp.bfloat16
    )
    return jnp.dot(hidden, down_piece, preferred_element_type=jnp.float32)


def on_device(
    queries, keys, values, log_decay, out_gain, out_proj, experts, gates, up_weight, down_weight
):
    highest = lax.Precision.HIGHEST
    ep_count = lax.axis_size("ep")
    heads_local = log_decay.shape[1]
    head_dim = queries.shape[1] // (heads_local * ep_count)
    query_heads, key_heads, value_heads = (
        lax.all_to_all(queries, "ep", split_axis=1, concat_axis=0, tiled=True),
        lax.all_to_all(keys, "ep", split_axis=1, concat_axis=0, tiled=True),
        lax.all_to_all(values, "ep", split_axis=1, concat_axis=0, tiled=True),
    )
    seg_length = query_heads.shape[0]
    query_heads = query_heads.reshape(seg_length, heads_local, head_dim)
    key_heads = key_heads.reshape(seg_length, heads_local, head_dim)
    value_heads = value_heads.reshape(seg_length, heads_local, head_dim)
    cumulative = jnp.cumsum(log_decay, axis=0)
    across = cumulative.T
    block_size = math.gcd(seg_length, 512)
    starts = jnp.arange(seg_length // block_size, dtype=jnp.int32) * block_size
    token_positions = jnp.arange(seg_length, dtype=jnp.int32)

    def block_mix(start):
        query_block = lax.dynamic_slice_in_dim(query_heads, start, block_size, 0)
        cum_block = lax.dynamic_slice_in_dim(across, start, block_size, 1)
        row_ids = start + jnp.arange(block_size, dtype=jnp.int32)
        causal = (row_ids[:, None] >= token_positions[None, :])[None]
        log_gap = cum_block[:, :, None] - across[:, None, :]
        weight = jnp.where(causal, jnp.exp(jnp.where(causal, log_gap, 0.0)), 0.0)
        scores = jnp.einsum(
            "thd,shd->hts", query_block, key_heads, preferred_element_type=jnp.float32
        )
        mixing = (scores * weight).astype(jnp.bfloat16)
        return jnp.einsum("hts,she->the", mixing, value_heads, preferred_element_type=jnp.float32)

    inside = lax.map(block_mix, starts).reshape(seg_length, heads_local, head_dim)
    ending = cumulative[-1]
    to_end = jnp.exp(ending[None, :] - cumulative)
    key_float = key_heads.astype(jnp.float32)
    value_float = value_heads.astype(jnp.float32)
    local_state = jnp.einsum("sh,shd,she->hde", to_end, key_float, value_float, precision=highest)
    identity = (jnp.ones_like(ending), jnp.zeros_like(local_state))
    carried = prefix((jnp.exp(ending), local_state), "seg", chain_combine, identity)[1]
    outside = jnp.exp(cumulative)[:, :, None] * jnp.einsum(
        "thd,hde->the", query_heads.astype(jnp.float32), carried, precision=highest
    )
    mixture = (inside + outside).astype(jnp.bfloat16).reshape(seg_length, heads_local * head_dim)
    token_mix = lax.all_to_all(mixture, "ep", split_axis=0, concat_axis=1, tiled=True)
    as_float = token_mix.astype(jnp.float32)
    inv_rms = lax.rsqrt(jnp.mean(as_float * as_float, axis=1, keepdims=True) + epsilon)
    attn_out = (as_float * inv_rms * out_gain[None, :]).astype(jnp.bfloat16)
    row_stride = 8
    own_width = heads_local * head_dim
    feature_count = own_width * ep_count
    picked_float = mixture.reshape(seg_length // row_stride, row_stride, own_width)[:, 0].astype(
        jnp.float32
    )
    square_sums = lax.psum(jnp.sum(picked_float * picked_float, axis=1), "ep")
    picked_rms = lax.rsqrt(square_sums[:, None] / feature_count + epsilon)
    gain_slice = lax.dynamic_slice_in_dim(out_gain, lax.axis_index("ep") * own_width, own_width, 0)
    normed_rows = (picked_float * picked_rms * gain_slice[None, :]).astype(jnp.bfloat16)
    proj_terms = jnp.dot(
        normed_rows,
        lax.all_gather(out_proj, "seg", axis=1, tiled=True),
        preferred_element_type=jnp.float32,
    )
    moe_in = lax.psum_scatter(
        proj_terms.astype(jnp.bfloat16), "ep", scatter_dimension=0, tiled=True
    )
    expert_count = ep_count // 2
    token_count, model_width = moe_in.shape
    capacity = max(2, 4 * token_count // expert_count)
    dispatch, combine = route_tables(experts, gates, expert_count, capacity)
    up_piece = up_weight[0]
    down_piece = down_weight[0]
    slot_rows = jnp.dot(dispatch, moe_in, preferred_element_type=jnp.float32).astype(jnp.bfloat16)
    outgoing = jnp.repeat(slot_rows.reshape(expert_count, capacity, model_width), 2, axis=0)
    arrived = lax.all_to_all(outgoing, "ep", split_axis=0, concat_axis=0, tiled=True).reshape(
        ep_count * capacity, model_width
    )
    gathered = lax.all_gather(arrived, "seg", axis=0, tiled=True)
    owned_sums = lax.psum_scatter(
        expert_output(gathered, up_piece, down_piece).astype(jnp.bfloat16),
        "seg",
        scatter_dimension=0,
        tiled=True,
    ).astype(jnp.float32)
    returned_back = lax.all_to_all(
        owned_sums.reshape(ep_count, capacity, model_width).astype(jnp.bfloat16),
        "ep",
        split_axis=0,
        concat_axis=0,
        tiled=True,
    ).astype(jnp.float32)
    paired = returned_back.reshape(expert_count, 2, capacity, model_width)
    halves = (paired[:, 0] + paired[:, 1]).reshape(expert_count * capacity, model_width)
    summed = jnp.dot(combine, halves, precision=highest)
    moe_out = summed.astype(jnp.bfloat16)
    return (attn_out, moe_out)


def solution(mesh):
    placed = (
        P(("seg", "ep"), None),
        P(("seg", "ep"), None),
        P(("seg", "ep"), None),
        P("seg", "ep"),
        P(),
        P("ep", "seg"),
        P(("seg", "ep"), None),
        P(("seg", "ep"), None),
        P("ep", None, "seg"),
        P("ep", "seg", None),
    )
    return jax.shard_map(
        on_device,
        mesh=mesh,
        in_specs=placed,
        out_specs=(P(("seg", "ep"), None), P(("seg", "ep"), None)),
        check_vma=False,
    )
```

profile of v0, /device:TPU:0, one launch (start us, length us, event | category | flops | bytes accessed | tf_op | source)
XLA Modules:
  0.0 282.9 jit_solution(439262611105810195)
XLA Ops:
  7.2 1.7 copy.181
  8.8 7.3 %all-to-all-start.1 = ((bf16[64,8,256]{2,0,1:T(8,128)(2,1)}), bf16[64,8,256]{2,0,1:T(8,128)(2,1)S(1)}, u32[]{:S(2)}, u32[]{:S(2)}) async-start(bf16[64,8,256]{2,0,1:T(8,128)(2,1)} %bitcast.87), calls=%async_computation.1 | async-start | bytes 524288 | tf_op jit(solution)/shard_map/all_to_all | solution.py:69
  16.1 1.7 copy.180
  17.8 7.2 %all-to-all-done.1 = bf16[64,8,256]{2,0,1:T(8,128)(2,1)S(1)} async-done(((bf16[64,8,256]{2,0,1:T(8,128)(2,1)}), bf16[64,8,256]{2,0,1:T(8,128)(2,1)S(1)}, u32[]{:S(2)}, u32[]{:S(2)}) %all-to-all-start.1) | async-done | bytes 262176 | tf_op jit(solution)/shard_map/all_to_all | solution.py:69
  25.0 3.6 %all-to-all-start.2 = ((bf16[64,8,256]{2,0,1:T(8,128)(2,1)}), bf16[64,8,256]{2,0,1:T(8,128)(2,1)S(1)}, u32[]{:S(2)}, u32[]{:S(2)}) async-start(bf16[64,8,256]{2,0,1:T(8,128)(2,1)} %bitcast.86), calls=%async_computation.2 | async-start | bytes 524288 | tf_op jit(solution)/shard_map/all_to_all | solution.py:70
  28.7 0.7 all-gather.5.cloned.1.call-update
  29.4 0.7 reshape.132
  30.1 0.6 reduce-window.6
  31.1 1.7 copy.182
  32.8 4.4 %all-to-all-done.2 = bf16[64,8,256]{2,0,1:T(8,128)(2,1)S(1)} async-done(((bf16[64,8,256]{2,0,1:T(8,128)(2,1)}), bf16[64,8,256]{2,0,1:T(8,128)(2,1)S(1)}, u32[]{:S(2)}, u32[]{:S(2)}) %all-to-all-start.2) | async-done | bytes 262176 | tf_op jit(solution)/shard_map/all_to_all | solution.py:70
  37.2 3.6 %all-to-all-start = ((bf16[64,8,256]{2,0,1:T(8,128)(2,1)}), bf16[64,8,256]{2,0,1:T(8,128)(2,1)S(1)}, u32[]{:S(2)}, u32[]{:S(2)}) async-start(bf16[64,8,256]{2,0,1:T(8,128)(2,1)} %bitcast.88), calls=%async_computation | async-start | bytes 524288 | tf_op jit(solution)/shard_map/all_to_all | solution.py:68
  41.0 5.2 %all-gather.1 = bf16[4,1,2]{2,1,0:T(2,128)(2,1)S(1)} all-gather(bf16[1,1,2]{2,1,0:T(2,128)(2,1)S(1)} %bitcast.114), channel_id=1, replica_groups=mesh['seg'=4,'ep'=8] {'seg'}, dimensions={0}, use_global_device_ids=true | all-gather | bytes 20 | tf_op jit(solution)/shard_map/all_gather | solution.py:13
  47.1 2.3 all-to-all-done
  49.4 0.6 convert_multiply_fusion.1
  50.0 0.6 convolution_convert_fusion.4
  50.6 7.7 %all-gather = bf16[8,128,128]{2,1,0:T(8,128)(2,1)S(1)} all-gather(bf16[2,128,128]{2,1,0:T(8,128)(2,1)S(1)} %convolution_convert_fusion.4), channel_id=2, replica_groups=mesh['seg'=4,'ep'=8] {'seg'}, dimensions={0}, use_global_device_ids=true | all-gather | bytes 327680 | tf_op jit(solution)/shard_map/all_gather | solution.py:13
  58.3 1.0 fusion.5
  59.4 0.4 fusion.8
  59.8 0.3 copy.138
  60.4 19.6 %psum.7 = f32[64]{0:T(128)S(1)} all-reduce(f32[64]{0:T(128)S(1)} %fusion.30), channel_id=1, replica_groups=mesh['seg'=4,'ep'=8] {'ep'}, use_global_device_ids=true, to_apply=%region_10.11 | all-reduce | flops 64 | bytes 512 | tf_op jit(solution)/shard_map/psum | solution.py:117
  80.0 3.5 %convolution_convert_fusion.1 = bf16[64,6144]{1,0:T(8,128)(2,1)} fusion(bf16[256,6144]{1,0:T(8,128)(2,1)} %all-gather.5.cloned.1.call-done, f32[64,1,256]{2,1,0:T(1,128)S(1)} %slice_convert_fusion, f32[256]{0:T(256)S(1)} %dynamic_slice.20, f32[64]{0:T(128)S(1)} %add_rsqrt_fusion), kind=kOutput, calls=%fused_computation.7 | convolution fusion | flops 201768960 | bytes 3998976 | tf_op jit(solution)/shard_map/dot_general | solution.py:121
  84.3 60.6 %reduce-scatter.3.cloned.1.call-done = bf16[8,6144]{1,0:T(8,128)(2,1)} async-done(((bf16[64,6144]{1,0:T(8,128)(2,1)}), bf16[8,6144]{1,0:T(8,128)(2,1)}) %reduce-scatter.3.cloned.1.call-update) | async-done | bytes 98320 | tf_op jit(solution)/shard_map/reduce_scatter | solution.py:126
  144.8 1.2 fusion.3
  146.1 21.9 %all_to_all.71 = bf16[8,8,6144]{2,1,0:T(8,128)(2,1)} all-to-all(bf16[8,8,6144]{2,1,0:T(8,128)(2,1)S(1)} %bitcast.97), channel_id=1, replica_groups=mesh['seg'=4,'ep'=8] {'ep'}, dimensions={0} | all-to-all | bytes 1572864 | tf_op jit(solution)/shard_map/all_to_all | solution.py:137
  168.2 27.4 %all-gather.7.cloned.1.call-done = bf16[256,6144]{1,0:T(8,128)(2,1)} async-done(((bf16[64,6144]{1,0:T(8,128)(2,1)}), bf16[256,6144]{1,0:T(8,128)(2,1)}) %all-gather.7.cloned.1.call-update) | async-done | bytes 3145744 | tf_op jit(solution)/shard_map/all_gather | solution.py:140
  195.6 15.9 %convolution_convert_fusion = bf16[256,6144]{1,0:T(8,128)(2,1)} fusion(bf16[1,576,6144]{2,1,0:T(8,128)(2,1)} %param.21, bf16[256,6144]{1,0:T(8,128)(2,1)} %all-gather.7.cloned.1.call-done, bf16[1,6144,576]{1,2,0:T(8,128)(2,1)} %param.20), kind=kOutput, calls=%fused_computation.3 | convolution fusion | flops 3626188800 | bytes 20447232 | tf_op jit(solution)/shard_map/dot_general | solution.py:57
  211.7 14.6 %all_to_all.72 = bf16[8,64,256]{2,1,0:T(8,128)(2,1)S(1)} all-to-all(bf16[8,64,256]{2,1,0:T(8,128)(2,1)S(1)} %all_to_all.61), channel_id=1, replica_groups=mesh['seg'=4,'ep'=8] {'ep'}, dimensions={0} | all-to-all | bytes 524288 | tf_op jit(solution)/shard_map/all_to_all | solution.py:107
  226.3 23.2 %reduce-scatter.5.cloned.1.call-done = bf16[64,6144]{1,0:T(8,128)(2,1)} async-done(((bf16[256,6144]{1,0:T(8,128)(2,1)}), bf16[64,6144]{1,0:T(8,128)(2,1)}) %reduce-scatter.5.cloned.1.call-update) | async-done | bytes 786448 | tf_op jit(solution)/shard_map/reduce_scatter | solution.py:141
  249.5 5.5 %all-to-all-start.5 = ((bf16[8,8,6144]{2,1,0:T(8,128)(2,1)}), bf16[8,8,6144]{2,1,0:T(8,128)(2,1)S(1)}, u32[]{:S(2)}, u32[]{:S(2)}) async-start(bf16[8,8,6144]{2,1,0:T(8,128)(2,1)} %bitcast.104), calls=%async_computation.7 | async-start | bytes 1572864 | tf_op jit(solution)/shard_map/all_to_all | solution.py:147
  255.4 0.8 multiply_convert_fusion.2
  256.2 18.9 %all-to-all-done.5 = bf16[8,8,6144]{2,1,0:T(8,128)(2,1)S(1)} async-done(((bf16[8,8,6144]{2,1,0:T(8,128)(2,1)}), bf16[8,8,6144]{2,1,0:T(8,128)(2,1)S(1)}, u32[]{:S(2)}, u32[]{:S(2)}) %all-to-all-start.5) | async-done | bytes 786464 | tf_op jit(solution)/shard_map/all_to_all | solution.py:147
  275.2 1.2 convolution_convert_fusion.3
  (51 shorter events, 3.6 us)
Async XLA Ops:
  7.2 39.6 %copy-start = (f32[2048]{0:T(1024)S(1)}, f32[2048]{0:T(1024)}, u32[]{:S(2)}) copy-start(f32[2048]{0:T(1024)} %param.16) | copy-start | bytes 24580
  8.8 16.2 %all-to-all-start.1 = ((bf16[64,8,256]{2,0,1:T(8,128)(2,1)}), bf16[64,8,256]{2,0,1:T(8,128)(2,1)S(1)}, u32[]{:S(2)}, u32[]{:S(2)}) async-start(bf16[64,8,256]{2,0,1:T(8,128)(2,1)} %bitcast.87), calls=%async_computation.1 | async-start | bytes 524288 | tf_op jit(solution)/shard_map/all_to_all | solution.py:69
  25.0 12.2 %all-to-all-start.2 = ((bf16[64,8,256]{2,0,1:T(8,128)(2,1)}), bf16[64,8,256]{2,0,1:T(8,128)(2,1)S(1)}, u32[]{:S(2)}, u32[]{:S(2)}) async-start(bf16[64,8,256]{2,0,1:T(8,128)(2,1)} %bitcast.86), calls=%async_computation.2 | async-start | bytes 524288 | tf_op jit(solution)/shard_map/all_to_all | solution.py:70
  28.6 51.3 %all-gather.5.cloned.1.call-start = ((), (), s32[]{:S(2)}) async-start(), calls=%async_computation.8 | async-start | bytes 3932160 | tf_op jit(solution)/shard_map/all_gather | solution.py:123
  37.2 12.1 %all-to-all-start = ((bf16[64,8,256]{2,0,1:T(8,128)(2,1)}), bf16[64,8,256]{2,0,1:T(8,128)(2,1)S(1)}, u32[]{:S(2)}, u32[]{:S(2)}) async-start(bf16[64,8,256]{2,0,1:T(8,128)(2,1)} %bitcast.88), calls=%async_computation | async-start | bytes 524288 | tf_op jit(solution)/shard_map/all_to_all | solution.py:68
  40.8 104.1 %reduce-scatter.3.cloned.1.call-start = ((), (), s32[]{:S(2)}) async-start(), calls=%async_computation.9 | async-start | bytes 884736 | tf_op jit(solution)/shard_map/reduce_scatter | solution.py:126
  59.8 23.8 %copy-start.1 = (s32[8,2]{0,1:T(2,128)S(1)}, s32[8,2]{0,1:T(2,128)}, u32[]{:S(2)}) copy-start(s32[8,2]{0,1:T(2,128)} %param.18) | copy-start | bytes 196
  83.5 112.1 %all-gather.7.cloned.1.call-start = ((), (), s32[]{:S(2)}) async-start(), calls=%async_computation.10 | async-start | bytes 3932160 | tf_op jit(solution)/shard_map/all_gather | solution.py:140
  168.0 81.5 %reduce-scatter.5.cloned.1.call-start = ((), (), s32[]{:S(2)}) async-start(), calls=%async_computation.11 | async-start | bytes 3932160 | tf_op jit(solution)/shard_map/reduce_scatter | solution.py:141
  211.5 43.6 %copy-start.2 = (f32[8,2]{0,1:T(2,128)S(1)}, f32[8,2]{0,1:T(2,128)}, u32[]{:S(2)}) copy-start(f32[8,2]{0,1:T(2,128)} %param.19) | copy-start | bytes 196
  249.5 25.6 %all-to-all-start.5 = ((bf16[8,8,6144]{2,1,0:T(8,128)(2,1)}), bf16[8,8,6144]{2,1,0:T(8,128)(2,1)S(1)}, u32[]{:S(2)}, u32[]{:S(2)}) async-start(bf16[8,8,6144]{2,1,0:T(8,128)(2,1)} %bitcast.104), calls=%async_computation.7 | async-start | bytes 1572864 | tf_op jit(solution)/shard_map/all_to_all | solution.py:147
Sparse Core Ops, SparseCore 0:
  31.0 31.3 all-gather.4
  83.6 61.1 reduce-scatter.2
  168.1 27.4 all-gather.6
  211.6 37.8 reduce-scatter.4
where the time goes:
time: 284 us; the launch traced here: 283 us
  waiting for transfers between devices  145 us (51%)
  blocking collectives  69 us (24%)
  matrix products  23.7 us (8%)
  starting transfers between devices  20.3 us (7%)
  between operations  14 us (5%)
  local copies, waits for them, and re-layouts  7.68 us (3%)
  other arithmetic  3.54 us (1%)
    reduce_scatter x1, waiting for transfers between devices, on_device(): lax.psum_scatter(proj_terms.astype(jnp.bfloat16), 'ep', scatter_dimension...  60.6 us
    all_gather x1, waiting for transfers between devices, on_device(): gathered = lax.all_gather(arrived, 'seg', axis=0, tiled=True)  27.4 us
    reduce_scatter x1, waiting for transfers between devices, on_device(): lax.psum_scatter(expert_output(gathered, up_piece, down_piece).astype(jnp...  23.2 us
    all_to_all x1, blocking collectives, on_device(): lax.all_to_all(outgoing, 'ep', split_axis=0, concat_axis=0, tiled=True)  21.9 us
    psum x1, blocking collectives, on_device(): square_sums = lax.psum(jnp.sum(picked_float * picked_float, axis=1), 'ep')  19.6 us
    all_to_all x1, waiting for transfers between devices, on_device(): lax.all_to_all(owned_sums.reshape(ep_count, capacity, model_width).astype...  18.9 us
    dot_general x1, matrix products, expert_output(): return jnp.dot(hidden, down_piece, preferred_element_type=jnp.float32)  15.9 us
    all_to_all x1, blocking collectives, on_device(): lax.all_to_all(mixture, 'ep', split_axis=0, concat_axis=1, tiled=True)  14.6 us
  transfers between devices with their start and end apart: 8, of which 7 were waited for; matrix products, arithmetic and copies ran while one was open for 4% of the time, Pallas kernels for 0%

commit v1 on v0

--- a/solution.py
+++ b/solution.py
@@ -137,7 +137,12 @@
     arrived = lax.all_to_all(outgoing, "ep", split_axis=0, concat_axis=0, tiled=True).reshape(
         ep_count * capacity, model_width
     )
-    gathered = lax.all_gather(arrived, "seg", axis=0, tiled=True)
+    ring = [arrived]
+    for hop in range(3):
+        ring.append(lax.ppermute(ring[-1], "seg", [(dev, (dev + 1) % 4) for dev in range(4)]))
+    gathered = jnp.roll(
+        jnp.concatenate(ring[::-1], axis=0), (lax.axis_index("seg") + 1) * ring[0].shape[0], axis=0
+    )
     owned_sums = lax.psum_scatter(
         expert_output(gathered, up_piece, down_piece).astype(jnp.bfloat16),
         "seg",

time: 284 us -> 297 us (1.046)
  local copies, waits for them, and re-layouts: 7.68 us -> 15.9 us
  waiting for transfers between devices: 145 us -> 153 us
    ppermute x0 -> x3, waiting for transfers between devices: none -> 34.2 us  [on_device(): lax.ppermute(ring[-1], 'seg', [(dev, (dev + 1) % 4) for dev in range(4)])]
    all_gather x1 -> x0, waiting for transfers between devices: 27.4 us -> none  [on_device(): gathered = lax.all_gather(arrived, 'seg', axis=0, tiled=True)]
    unnamed x8 -> x15, local copies, waits for them, and re-layouts: 0.1 us -> 6.69 us
  transfers between devices with their start and end apart: 8 -> 10, of which waited for: 7 -> 9; matrix products, arithmetic and copies ran while one was open for 4% -> 4% of each run, Pallas kernels for 0% -> 0%
where the time goes in v1:
time: 297 us
  waiting for transfers between devices  153 us (52%)
  blocking collectives  66.6 us (22%)
  matrix products  23.7 us (8%)
  starting transfers between devices  20.1 us (7%)
  local copies, waits for them, and re-layouts  15.9 us (5%)
  between operations  13.9 us (5%)
  other arithmetic  3.54 us (1%)
    reduce_scatter x1, waiting for transfers between devices, on_device(): lax.psum_scatter(proj_terms.astype(jnp.bfloat16), 'ep', scatter_dimension...  60.5 us
    ppermute x3, waiting for transfers between devices, on_device(): lax.ppermute(ring[-1], 'seg', [(dev, (dev + 1) % 4) for dev in range(4)])  34.2 us
    reduce_scatter x1, waiting for transfers between devices, on_device(): lax.psum_scatter(expert_output(gathered, up_piece, down_piece).astype(jnp...  25.1 us
    all_to_all x1, blocking collectives, on_device(): lax.all_to_all(outgoing, 'ep', split_axis=0, concat_axis=0, tiled=True)  21.7 us
    psum x1, blocking collectives, on_device(): square_sums = lax.psum(jnp.sum(picked_float * picked_float, axis=1), 'ep')  20.3 us
    all_to_all x1, waiting for transfers between devices, on_device(): lax.all_to_all(owned_sums.reshape(ep_count, capacity, model_width).astype...  18.9 us
    dot_general x1, matrix products, expert_output(): return jnp.dot(hidden, down_piece, preferred_element_type=jnp.float32)  15.9 us
    all_gather x2, blocking collectives, prefix(): lax.all_gather(a.astype(kind), axis)  12.9 us
  transfers between devices with their start and end apart: 10, of which 9 were waited for; matrix products, arithmetic and copies ran while one was open for 4% of the time, Pallas kernels for 0%

profile of v1, /device:TPU:0, one launch (start us, length us, event | category | flops | bytes accessed | tf_op | source)
XLA Modules:
  0.0 296.6 jit_solution(9698633333152036990)
XLA Ops:
  7.2 1.7 copy.181
  8.8 7.3 %all-to-all-start.1 = ((bf16[64,8,256]{2,0,1:T(8,128)(2,1)}), bf16[64,8,256]{2,0,1:T(8,128)(2,1)S(1)}, u32[]{:S(2)}, u32[]{:S(2)}) async-start(bf16[64,8,256]{2,0,1:T(8,128)(2,1)} %bitcast.88), calls=%async_computation.1 | async-start | bytes 524288 | tf_op jit(solution)/shard_map/all_to_all | solution.py:69
  16.1 1.7 copy.180
  17.8 7.2 %all-to-all-done.1 = bf16[64,8,256]{2,0,1:T(8,128)(2,1)S(1)} async-done(((bf16[64,8,256]{2,0,1:T(8,128)(2,1)}), bf16[64,8,256]{2,0,1:T(8,128)(2,1)S(1)}, u32[]{:S(2)}, u32[]{:S(2)}) %all-to-all-start.1) | async-done | bytes 262176 | tf_op jit(solution)/shard_map/all_to_all | solution.py:69
  25.0 3.6 %all-to-all-start.2 = ((bf16[64,8,256]{2,0,1:T(8,128)(2,1)}), bf16[64,8,256]{2,0,1:T(8,128)(2,1)S(1)}, u32[]{:S(2)}, u32[]{:S(2)}) async-start(bf16[64,8,256]{2,0,1:T(8,128)(2,1)} %bitcast.87), calls=%async_computation.2 | async-start | bytes 524288 | tf_op jit(solution)/shard_map/all_to_all | solution.py:70
  31.1 1.7 copy.182
  32.8 4.4 %all-to-all-done.2 = bf16[64,8,256]{2,0,1:T(8,128)(2,1)S(1)} async-done(((bf16[64,8,256]{2,0,1:T(8,128)(2,1)}), bf16[64,8,256]{2,0,1:T(8,128)(2,1)S(1)}, u32[]{:S(2)}, u32[]{:S(2)}) %all-to-all-start.2) | async-done | bytes 262176 | tf_op jit(solution)/shard_map/all_to_all | solution.py:70
  37.2 3.6 %all-to-all-start = ((bf16[64,8,256]{2,0,1:T(8,128)(2,1)}), bf16[64,8,256]{2,0,1:T(8,128)(2,1)S(1)}, u32[]{:S(2)}, u32[]{:S(2)}) async-start(bf16[64,8,256]{2,0,1:T(8,128)(2,1)} %bitcast.89), calls=%async_computation | async-start | bytes 524288 | tf_op jit(solution)/shard_map/all_to_all | solution.py:68
  41.0 5.2 %all-gather.1 = bf16[4,1,2]{2,1,0:T(2,128)(2,1)S(1)} all-gather(bf16[1,1,2]{2,1,0:T(2,128)(2,1)S(1)} %bitcast.115), channel_id=1, replica_groups=mesh['seg'=4,'ep'=8] {'seg'}, dimensions={0}, use_global_device_ids=true | all-gather | bytes 20 | tf_op jit(solution)/shard_map/all_gather | solution.py:13
  47.7 1.6 all-to-all-done
  50.6 7.7 %all-gather = bf16[8,128,128]{2,1,0:T(8,128)(2,1)S(1)} all-gather(bf16[2,128,128]{2,1,0:T(8,128)(2,1)S(1)} %convolution_convert_fusion.4), channel_id=2, replica_groups=mesh['seg'=4,'ep'=8] {'seg'}, dimensions={0}, use_global_device_ids=true | all-gather | bytes 327680 | tf_op jit(solution)/shard_map/all_gather | solution.py:13
  58.3 1.0 fusion.6
  60.3 20.3 %psum.7 = f32[64]{0:T(128)S(1)} all-reduce(f32[64]{0:T(128)S(1)} %fusion.30), channel_id=1, replica_groups=mesh['seg'=4,'ep'=8] {'ep'}, use_global_device_ids=true, to_apply=%region_10.11 | all-reduce | flops 64 | bytes 512 | tf_op jit(solution)/shard_map/psum | solution.py:117
  80.6 3.5 %convolution_convert_fusion.1 = bf16[64,6144]{1,0:T(8,128)(2,1)} fusion(bf16[256,6144]{1,0:T(8,128)(2,1)} %all-gather.4.cloned.1.call-done, f32[64,1,256]{2,1,0:T(1,128)S(1)} %slice_convert_fusion, f32[256]{0:T(256)S(1)} %dynamic_slice.24, f32[64]{0:T(128)S(1)} %add_rsqrt_fusion), kind=kOutput, calls=%fused_computation.7 | convolution fusion | flops 201768960 | bytes 3998976 | tf_op jit(solution)/shard_map/dot_general | solution.py:121
  84.9 60.5 %reduce-scatter.3.cloned.1.call-done = bf16[8,6144]{1,0:T(8,128)(2,1)} async-done(((bf16[64,6144]{1,0:T(8,128)(2,1)}), bf16[8,6144]{1,0:T(8,128)(2,1)}) %reduce-scatter.3.cloned.1.call-update) | async-done | bytes 98320 | tf_op jit(solution)/shard_map/reduce_scatter | solution.py:126
  145.4 1.2 fusion.3
  146.6 21.7 %all_to_all.71 = bf16[8,8,6144]{2,1,0:T(8,128)(2,1)S(1)} all-to-all(bf16[8,8,6144]{2,1,0:T(8,128)(2,1)S(1)} %bitcast.98), channel_id=1, replica_groups=mesh['seg'=4,'ep'=8] {'ep'}, dimensions={0} | all-to-all | bytes 1572864 | tf_op jit(solution)/shard_map/all_to_all | solution.py:137
  168.4 11.4 %collective-permute-done = bf16[64,6144]{1,0:T(8,128)(2,1)S(1)} collective-permute-done((bf16[64,6144]{1,0:T(8,128)(2,1)S(1)}, bf16[64,6144]{1,0:T(8,128)(2,1)S(1)}, u32[]{:S(2)}, u32[]{:S(2)}) %collective-permute-start) | collective-permute-done | bytes 786464 | tf_op jit(solution)/shard_map/ppermute | solution.py:142
  179.8 11.4 %collective-permute-done.1 = bf16[64,6144]{1,0:T(8,128)(2,1)S(1)} collective-permute-done((bf16[64,6144]{1,0:T(8,128)(2,1)S(1)}, bf16[64,6144]{1,0:T(8,128)(2,1)S(1)}, u32[]{:S(2)}, u32[]{:S(2)}) %collective-permute-start.1) | collective-permute-done | bytes 786464 | tf_op jit(solution)/shard_map/ppermute | solution.py:142
  191.2 11.4 %collective-permute-done.2 = bf16[64,6144]{1,0:T(8,128)(2,1)S(1)} collective-permute-done((bf16[64,6144]{1,0:T(8,128)(2,1)S(1)}, bf16[64,6144]{1,0:T(8,128)(2,1)S(1)}, u32[]{:S(2)}, u32[]{:S(2)}) %collective-permute-start.2) | collective-permute-done | bytes 786464 | tf_op jit(solution)/shard_map/ppermute | solution.py:142
  203.6 1.0 constant_dynamic-update-slice_fusion.6
  204.5 0.9 constant_dynamic-update-slice_fusion.5
  205.5 0.9 constant_dynamic-update-slice_fusion.4
  206.4 0.9 constant_dynamic-update-slice_fusion.3
  208.3 0.9 constant_dynamic-update-slice_fusion.1
  209.2 1.0 constant_dynamic-update-slice_fusion
  210.2 15.9 %convolution_convert_fusion = bf16[256,6144]{1,0:T(8,128)(2,1)} fusion(bf16[1,576,6144]{2,1,0:T(8,128)(2,1)} %param.21, bf16[1,6144,576]{1,2,0:T(8,128)(2,1)} %param.20, bf16[512,6144]{1,0:T(8,128)(2,1)} %constant_dynamic-update-slice_fusion, s32[]{:T(128)S(6)} %select_n.44), kind=kOutput, calls=%fused_computation.3 | convolution fusion | flops 3626188800 | bytes 20447236 | tf_op jit(solution)/shard_map/dot_general | solution.py:57
  226.3 11.8 %all_to_all.72 = bf16[8,64,256]{2,1,0:T(8,128)(2,1)S(1)} all-to-all(bf16[8,64,256]{2,1,0:T(8,128)(2,1)S(1)} %all_to_all.61), channel_id=1, replica_groups=mesh['seg'=4,'ep'=8] {'ep'}, dimensions={0} | all-to-all | bytes 524288 | tf_op jit(solution)/shard_map/all_to_all | solution.py:107
  238.1 25.1 %reduce-scatter.5.cloned.1.call-done = bf16[64,6144]{1,0:T(8,128)(2,1)} async-done(((bf16[256,6144]{1,0:T(8,128)(2,1)}), bf16[64,6144]{1,0:T(8,128)(2,1)}) %reduce-scatter.5.cloned.1.call-update) | async-done | bytes 786448 | tf_op jit(solution)/shard_map/reduce_scatter | solution.py:146
  263.2 5.5 %all-to-all-start.5 = ((bf16[8,8,6144]{2,1,0:T(8,128)(2,1)}), bf16[8,8,6144]{2,1,0:T(8,128)(2,1)S(1)}, u32[]{:S(2)}, u32[]{:S(2)}) async-start(bf16[8,8,6144]{2,1,0:T(8,128)(2,1)} %bitcast.105), calls=%async_computation.7 | async-start | bytes 1572864 | tf_op jit(solution)/shard_map/all_to_all | solution.py:152
  269.9 18.9 %all-to-all-done.5 = bf16[8,8,6144]{2,1,0:T(8,128)(2,1)S(1)} async-done(((bf16[8,8,6144]{2,1,0:T(8,128)(2,1)}), bf16[8,8,6144]{2,1,0:T(8,128)(2,1)S(1)}, u32[]{:S(2)}, u32[]{:S(2)}) %all-to-all-start.5) | async-done | bytes 786464 | tf_op jit(solution)/shard_map/all_to_all | solution.py:152
  288.9 1.2 convolution_convert_fusion.3
  (62 shorter events, 10.6 us)
Async XLA Ops:
  8.8 16.2 %all-to-all-start.1 = ((bf16[64,8,256]{2,0,1:T(8,128)(2,1)}), bf16[64,8,256]{2,0,1:T(8,128)(2,1)S(1)}, u32[]{:S(2)}, u32[]{:S(2)}) async-start(bf16[64,8,256]{2,0,1:T(8,128)(2,1)} %bitcast.88), calls=%async_computation.1 | async-start | bytes 524288 | tf_op jit(solution)/shard_map/all_to_all | solution.py:69
  25.0 12.2 %all-to-all-start.2 = ((bf16[64,8,256]{2,0,1:T(8,128)(2,1)}), bf16[64,8,256]{2,0,1:T(8,128)(2,1)S(1)}, u32[]{:S(2)}, u32[]{:S(2)}) async-start(bf16[64,8,256]{2,0,1:T(8,128)(2,1)} %bitcast.87), calls=%async_computation.2 | async-start | bytes 524288 | tf_op jit(solution)/shard_map/all_to_all | solution.py:70
  28.6 52.0 %all-gather.4.cloned.1.call-start = ((), (), s32[]{:S(2)}) async-start(), calls=%async_computation.8 | async-start | bytes 3932160 | tf_op jit(solution)/shard_map/all_gather | solution.py:123
  37.2 12.1 %all-to-all-start = ((bf16[64,8,256]{2,0,1:T(8,128)(2,1)}), bf16[64,8,256]{2,0,1:T(8,128)(2,1)S(1)}, u32[]{:S(2)}, u32[]{:S(2)}) async-start(bf16[64,8,256]{2,0,1:T(8,128)(2,1)} %bitcast.89), calls=%async_computation | async-start | bytes 524288 | tf_op jit(solution)/shard_map/all_to_all | solution.py:68
  40.8 104.6 %reduce-scatter.3.cloned.1.call-start = ((), (), s32[]{:S(2)}) async-start(), calls=%async_computation.9 | async-start | bytes 884736 | tf_op jit(solution)/shard_map/reduce_scatter | solution.py:126
  58.3 25.9 %copy-start.1 = (s32[8,2]{0,1:T(2,128)S(1)}, s32[8,2]{0,1:T(2,128)}, u32[]{:S(2)}) copy-start(s32[8,2]{0,1:T(2,128)} %param.18) | copy-start | bytes 196
  84.1 179.1 %reduce-scatter.5.cloned.1.call-start = ((), (), s32[]{:S(2)}) async-start(), calls=%async_computation.10 | async-start | bytes 3932160 | tf_op jit(solution)/shard_map/reduce_scatter | solution.py:146
  168.4 11.4 %collective-permute-start = (bf16[64,6144]{1,0:T(8,128)(2,1)S(1)}, bf16[64,6144]{1,0:T(8,128)(2,1)S(1)}, u32[]{:S(2)}, u32[]{:S(2)}) collective-permute-start(bf16[64,6144]{1,0:T(8,128)(2,1)S(1)} %bitcast.97), channel_id=1, source_target_pairs={{0,8},{8,16},{16,24},{24,0},{1,9},{9,17},{17,25},{25,1},{2,10},{10... | collective-permute-start | bytes 2359304 | tf_op jit(solution)/shard_map/ppermute | solution.py:142
  179.8 11.4 %collective-permute-start.1 = (bf16[64,6144]{1,0:T(8,128)(2,1)S(1)}, bf16[64,6144]{1,0:T(8,128)(2,1)S(1)}, u32[]{:S(2)}, u32[]{:S(2)}) collective-permute-start(bf16[64,6144]{1,0:T(8,128)(2,1)S(1)} %collective-permute-done), channel_id=1, source_target_pairs={{0,8},{8,16},{16,24},{24,0},{1,9},{9,17},{17,25},{25,1},{2,10},{10... | collective-permute-start | bytes 2359304 | tf_op jit(solution)/shard_map/ppermute | solution.py:142
  191.2 11.4 %collective-permute-start.2 = (bf16[64,6144]{1,0:T(8,128)(2,1)S(1)}, bf16[64,6144]{1,0:T(8,128)(2,1)S(1)}, u32[]{:S(2)}, u32[]{:S(2)}) collective-permute-start(bf16[64,6144]{1,0:T(8,128)(2,1)S(1)} %collective-permute-done.1), channel_id=1, source_target_pairs={{0,8},{8,16},{16,24},{24,0},{1,9},{9,17},{17,25},{25,1},{2,10},{10... | collective-permute-start | bytes 2359304 | tf_op jit(solution)/shard_map/ppermute | solution.py:142
  210.2 58.5 %copy-start.2 = (f32[8,2]{0,1:T(2,128)S(1)}, f32[8,2]{0,1:T(2,128)}, u32[]{:S(2)}) copy-start(f32[8,2]{0,1:T(2,128)} %param.19) | copy-start | bytes 196
  226.1 42.9 %copy-start = (f32[2048]{0:T(1024)S(1)}, f32[2048]{0:T(1024)}, u32[]{:S(2)}) copy-start(f32[2048]{0:T(1024)} %param.16) | copy-start | bytes 24580
  263.2 25.6 %all-to-all-start.5 = ((bf16[8,8,6144]{2,1,0:T(8,128)(2,1)}), bf16[8,8,6144]{2,1,0:T(8,128)(2,1)S(1)}, u32[]{:S(2)}, u32[]{:S(2)}) async-start(bf16[8,8,6144]{2,1,0:T(8,128)(2,1)} %bitcast.105), calls=%async_computation.7 | async-start | bytes 1572864 | tf_op jit(solution)/shard_map/all_to_all | solution.py:152
Sparse Core Ops, SparseCore 0:
  31.0 31.3 all-gather.3
  84.2 61.1 reduce-scatter.2
  226.2 36.8 reduce-scatter.4
